TPU v7x, 128 devices: a whole 4x4x4 slice. The times are simulated.
128 devices in a mesh: replica: 16 (over z, y), tensor: 8 (over x, core).
Axes of the slice: x: 4, y: 4, z: 4, core: 2. Of those that a mesh axis runs over, the one named last changes fastest.
Arguments:
- attended: bfloat16 [16384, 8192], P('replica', 'tensor'), may hold values from -6 to 6
- out_weight: bfloat16 [8192, 8192], P('tensor'), may hold values from -0.09375 to 0.09375
- shrink_weight: bfloat16 [192, 64, 8192], P('replica', None, 'tensor'), may hold values from -0.0625 to 0.0625
- expand_weight: bfloat16 [192, 64, 8192], P('replica', None, 'tensor'), may hold values from -0.75 to 0.75
- block_adapter: int32 [128], P('replica'), may hold values from 0 to 191, as said below
- block_fill: int32 [128], P('replica'), may hold values from 1 to 128
Outputs:
- projected: bfloat16 [16384, 8192], P('replica', 'tensor')
Inputs may be any that keep to these rules, and one draw needn't show every extreme that they name: `block_adapter`: the owner of adapter j is replica j // 12. Among the 8 blocks of one replica, at most 1 have adapters of one owner; one owner gets exactly 1 block from every replica.
All inputs are finite; a program needn't handle non-finite values.
Results may differ from a plain program's by a relative error of at most 0.02.
Values may be sent and summed in bfloat16 or wider, within the bound.
No kernel may reach another device: no remote copies, remote signals or barrier semaphores. Data moves between devices by JAX's collectives and lax.ppermute only.
A program may use at most 128 MiB of HBM per device.

v0:
```python
import jax
import jax.numpy as jnp
from jax import lax
from jax.sharding import PartitionSpec as P


def slot_layout(block_ids, per_owner, capacity):
    block_owner = block_ids // per_owner
    local_ids = block_ids - block_owner * per_owner
    positions = jnp.arange(block_ids.shape[-1])
    earlier_same = (block_owner[..., None, :] == block_owner[..., :, None]) & (
        positions[None, :] < positions[:, None]
    )
    slot_rank = jnp.sum(earlier_same.astype(jnp.int32), axis=-1)
    return (block_owner * capacity + slot_rank, local_ids)


def local(attended, out_weight, shrink_weight, expand_weight, block_adapter, block_fill):
    tok_rows, feature_piece = attended.shape
    block_count = block_adapter.shape[0]
    block_rows = tok_rows // block_count
    owner_count = lax.axis_size("replica")
    capacity = max(1, (2 * block_count + owner_count - 1) // owner_count)
    per_owner = shrink_weight.shape[0]
    slot_count = owner_count * capacity
    slot_index, local_ids = slot_layout(block_adapter, per_owner, capacity)
    block_table = lax.all_gather(block_adapter, "replica", axis=0, tiled=True).reshape(
        owner_count, block_count
    )
    all_slots, all_local = slot_layout(block_table, per_owner, capacity)
    wanted_slot = lax.axis_index("replica") * capacity + jnp.arange(capacity)
    served_hit = all_slots[:, None, :] == wanted_slot[None, :, None]
    served_ids = jnp.sum(jnp.where(served_hit, all_local[:, None, :], 0), axis=-1)
    row_blocks = attended.reshape(block_count, block_rows, feature_piece)
    slot_match = jnp.arange(slot_count)[:, None] == slot_index[None, :]
    slot_source = jnp.sum(jnp.where(slot_match, jnp.arange(block_count)[None, :], 0), axis=1)
    slot_filled = jnp.any(slot_match, axis=1)
    outgoing = jnp.where(slot_filled[:, None, None], row_blocks[slot_source], 0)
    outgoing = outgoing.reshape(owner_count, capacity, block_rows, feature_piece)
    arrived = lax.all_to_all(outgoing, "replica", split_axis=0, concat_axis=0, tiled=True)
    partial_low = jnp.einsum(
        "scbp,scrp->scrb", arrived, shrink_weight[served_ids], preferred_element_type=jnp.float32
    )
    low_rank = lax.psum(partial_low.astype(jnp.bfloat16), "tensor")
    delta_slots = jnp.einsum(
        "scrb,scrp->scbp", low_rank, expand_weight[served_ids], preferred_element_type=jnp.float32
    ).astype(jnp.bfloat16)
    returned = lax.all_to_all(delta_slots, "replica", split_axis=0, concat_axis=0, tiled=True)
    delta_rows = returned.reshape(slot_count, block_rows, feature_piece)[slot_index]
    partial_out = jnp.dot(attended, out_weight, preferred_element_type=jnp.float32)
    base_out = lax.psum_scatter(
        partial_out.astype(jnp.bfloat16), "tensor", scatter_dimension=1, tiled=True
    ).astype(jnp.float32)
    combined = base_out.reshape(block_count, block_rows, feature_piece) + delta_rows.astype(
        jnp.float32
    )
    live_rows = jnp.arange(block_rows)[None, :] < block_fill[:, None]
    projected = jnp.where(live_rows[:, :, None], combined, 0.0).astype(jnp.bfloat16)
    return projected.reshape(tok_rows, feature_piece)


def solution(mesh):
    in_specs = (
        P("replica", "tensor"),
        P("tensor", None),
        P("replica", None, "tensor"),
        P("replica", None, "tensor"),
        P("replica"),
        P("replica"),
    )
    out_specs = P("replica", "tensor")
    return jax.shard_map(local, mesh=mesh, in_specs=in_specs, out_specs=out_specs, check_vma=False)
```

profile of v0, /device:TPU:1, one launch (start us, length us, event | category | flops | bytes accessed | tf_op | source)
XLA Modules:
  0.0 267.1 jit_solution(30264454527374163)
XLA Ops:
  6.5 0.8 and_select_fusion
  7.4 0.2 convert_reduce_fusion.1
  7.5 0.7 compare_select_fusion
  8.2 0.1 select_reduce_fusion
  8.3 0.1 fusion.7
  8.4 0.0 copy-done
  8.4 2.8 %gather_fusion.1 = bf16[16,128,1024]{2,1,0:T(8,128)(2,1)} fusion(bf16[8,128,1024]{2,1,0:T(8,128)(2,1)S(1)} %bitcast.32, s32[1024]{0:T(1024)S(1)} %pad_clamp_fusion.1), kind=kCustom, calls=%fused_computation.1 | custom fusion | bytes 8388672 | tf_op jit(solution)/shard_map/gather | solution.py:38
  11.2 4.5 %bitcast_select_fusion = bf16[16,1,128,1024]{3,2,1,0:T(8,128)(2,1)} fusion(bf16[16,128,1024]{2,1,0:T(8,128)(2,1)} %gather_fusion.1, pred[16]{0:T(512)(128)(4,1)S(1)} %fusion.7), kind=kLoop, calls=%fused_computation.10 | loop fusion | flops 2097152 | bytes 8388624 | tf_op jit(solution)/shard_map/jit(_where)/select_n | solution.py:38
  15.7 8.8 %all-to-all-start = ((bf16[16,1,128,1024]{3,2,1,0:T(8,128)(2,1)}), bf16[16,1,128,1024]{3,2,1,0:T(8,128)(2,1)}, u32[]{:S(2)}, u32[]{:S(2)}) async-start(bf16[16,1,128,1024]{3,2,1,0:T(8,128)(2,1)} %bitcast_select_fusion), calls=%async_computation.1 | async-start | bytes 8388608 | tf_op jit(solution)/shard_map/all_to_all | solution.py:40
  24.5 0.0 all-reduce.3.cloned.1.call-start
  24.5 0.6 dynamic-slice
  25.8 0.2 dynamic-update-slice
  26.0 64.7 %all-reduce = s32[128]{0:T(128)S(1)} all-reduce(s32[128]{0:T(128)S(1)} %dynamic-update-slice), channel_id=1, replica_groups=mesh['replica'=16,'tensor'=8] {'replica'}, use_global_device_ids=true, to_apply=%add | all-reduce | flops 128 | bytes 1024
  90.8 0.1 reshape.153
  90.9 0.1 copy.8
  91.0 0.1 convert_reduce_fusion
  91.1 3.4 %gather_fusion = bf16[16,64,1024]{2,1,0:T(8,128)(2,1)} fusion(bf16[12,64,1024]{2,1,0:T(8,128)(2,1)} %param.8, s32[1024]{0:T(1024)S(1)} %pad_clamp_fusion.2), kind=kCustom, calls=%fused_computation | custom fusion | bytes 4194368 | tf_op jit(solution)/shard_map/gather | solution.py:42
  94.5 0.0 all-to-all-done
  94.5 5.1 %fusion.4 = bf16[16,64,128]{2,1,0:T(8,128)(2,1)} fusion(bf16[16,64,1024]{2,1,0:T(8,128)(2,1)} %gather_fusion, bf16[16,1,128,1024]{3,2,1,0:T(8,128)(2,1)} %all-to-all-done), kind=kOutput, calls=%fused_computation.12 | convolution fusion | flops 268566528 | bytes 6553600 | tf_op jit(solution)/shard_map/scbp,scrp->scrb/dot_general | solution.py:41
  99.6 0.0 all-reduce.3.cloned.1.call-update
  99.6 0.0 reduce-scatter.2.cloned.1.call-start
  99.7 25.8 %convolution_convert_fusion = bf16[1024,8192]{1,0:T(8,128)(2,1)} fusion(bf16[1024,1024]{1,0:T(8,128)(2,1)S(1)} %copy-done, bf16[1024,8192]{1,0:T(8,128)(2,1)} %param.7), kind=kOutput, calls=%fused_computation.4 | convolution fusion | flops 17188257792 | bytes 35651584 | tf_op jit(solution)/shard_map/dot_general | solution.py:50
  125.5 0.0 reduce-scatter.2.cloned.1.call-update
  125.5 2.1 gather_fusion.2
  127.6 33.4 %all-reduce.3.cloned.1.call-done = bf16[16,64,128]{2,1,0:T(8,128)(2,1)} async-done(((bf16[16,64,128]{2,1,0:T(8,128)(2,1)}), bf16[16,64,128]{2,1,0:T(8,128)(2,1)}) %all-reduce.3.cloned.1.call-update) | async-done | bytes 262160 | tf_op jit(solution)/shard_map/psum | solution.py:44
  161.0 4.2 %convert_bitcast_fusion = bf16[16,1,128,1024]{3,2,1,0:T(8,128)(2,1)} fusion(bf16[16,64,128]{2,1,0:T(8,128)(2,1)} %all-reduce.3.cloned.1.call-done, bf16[16,64,1024]{2,1,0:T(8,128)(2,1)S(1)} %gather_fusion.2), kind=kOutput, calls=%fused_computation.11 | convolution fusion | flops 270532608 | bytes 6553600 | tf_op jit(solution)/shard_map/scrb,scrp->scbp/dot_general | solution.py:45
  165.2 6.9 %all-to-all-start.1 = ((bf16[16,1,128,1024]{3,2,1,0:T(8,128)(2,1)}), bf16[16,1,128,1024]{3,2,1,0:T(8,128)(2,1)}, u32[]{:S(2)}, u32[]{:S(2)}) async-start(bf16[16,1,128,1024]{3,2,1,0:T(8,128)(2,1)} %convert_bitcast_fusion), calls=%async_computation.2 | async-start | bytes 8388608 | tf_op jit(solution)/shard_map/all_to_all | solution.py:48
  172.1 0.1 fusion.8
  172.2 55.8 %all-to-all-done.1 = bf16[16,1,128,1024]{3,2,1,0:T(8,128)(2,1)} async-done(((bf16[16,1,128,1024]{3,2,1,0:T(8,128)(2,1)}), bf16[16,1,128,1024]{3,2,1,0:T(8,128)(2,1)}, u32[]{:S(2)}, u32[]{:S(2)}) %all-to-all-start.1) | async-done | bytes 4194336 | tf_op jit(solution)/shard_map/all_to_all | solution.py:48
  228.0 4.4 %gather_fusion.3 = bf16[8,128,1024]{2,1,0:T(8,128)(2,1)} fusion(bf16[16,128,1024]{2,1,0:T(8,128)(2,1)} %bitcast.11, s32[1024]{0:T(1024)S(1)} %pad_clamp_fusion), kind=kCustom, calls=%fused_computation.3 | custom fusion | bytes 4194336 | tf_op jit(solution)/shard_map/gather | solution.py:49
  232.4 23.6 %reduce-scatter.2.cloned.1.call-done = bf16[1024,1024]{1,0:T(8,128)(2,1)} async-done(((bf16[1024,8192]{1,0:T(8,128)(2,1)}), bf16[1024,1024]{1,0:T(8,128)(2,1)}) %reduce-scatter.2.cloned.1.call-update) | async-done | bytes 2097168 | tf_op jit(solution)/shard_map/reduce_scatter | solution.py:51
  256.0 4.2 %fusion.1 = bf16[1024,1024]{1,0:T(8,128)(2,1)} fusion(bf16[1024,1024]{1,0:T(8,128)(2,1)} %reduce-scatter.2.cloned.1.call-done, bf16[8,128,1024]{2,1,0:T(8,128)(2,1)} %gather_fusion.3, pred[1024]{0:T(1024)(128)(4,1)S(1)} %fusion.8), kind=kLoop, calls=%fused_computation.7 | loop fusion | flops 5242880 | bytes 6292480 | tf_op jit(solution)/shard_map/convert_element_type | solution.py:58
  (18 shorter events, 0.1 us)
Async XLA Ops:
  6.5 1.9 copy-start
  15.7 8.9 %copy-start.4 = (u32[128]{0:T(128)S(1)}, u32[128]{0:T(128)}, u32[]{:S(2)}) copy-start(u32[128]{0:T(128)} %constant.44) | copy-start | bytes 1540
  15.7 10.1 %copy-start.2 = (s32[8]{0:T(128)S(1)}, s32[8]{0:T(128)}, u32[]{:S(2)}) copy-start(s32[8]{0:T(128)} %param.10) | copy-start | bytes 100
  15.7 78.8 %all-to-all-start = ((bf16[16,1,128,1024]{3,2,1,0:T(8,128)(2,1)}), bf16[16,1,128,1024]{3,2,1,0:T(8,128)(2,1)}, u32[]{:S(2)}, u32[]{:S(2)}) async-start(bf16[16,1,128,1024]{3,2,1,0:T(8,128)(2,1)} %bitcast_select_fusion), calls=%async_computation.1 | async-start | bytes 8388608 | tf_op jit(solution)/shard_map/all_to_all | solution.py:40
  24.5 136.5 %all-reduce.3.cloned.1.call-start = ((), (), s32[]{:S(2)}) async-start(), calls=%async_computation.4 | async-start | bytes 524288 | tf_op jit(solution)/shard_map/psum | solution.py:44
  99.6 156.4 %reduce-scatter.2.cloned.1.call-start = ((), (), s32[]{:S(2)}) async-start(), calls=%async_computation.3 | async-start | bytes 18874368 | tf_op jit(solution)/shard_map/reduce_scatter | solution.py:51
  165.2 6.9 %copy-start.3 = (s32[8]{0:T(128)S(1)}, s32[8]{0:T(128)}, u32[]{:S(2)}) copy-start(s32[8]{0:T(128)} %param.11) | copy-start | bytes 100
  165.2 62.8 %all-to-all-start.1 = ((bf16[16,1,128,1024]{3,2,1,0:T(8,128)(2,1)}), bf16[16,1,128,1024]{3,2,1,0:T(8,128)(2,1)}, u32[]{:S(2)}, u32[]{:S(2)}) async-start(bf16[16,1,128,1024]{3,2,1,0:T(8,128)(2,1)} %convert_bitcast_fusion), calls=%async_computation.2 | async-start | bytes 8388608 | tf_op jit(solution)/shard_map/all_to_all | solution.py:48
  228.0 32.2 %copy-start.1 = (bf16[1024,1024]{1,0:T(8,128)(2,1)S(1)}, bf16[1024,1024]{1,0:T(8,128)(2,1)}, u32[]{:S(2)}) copy-start(bf16[1024,1024]{1,0:T(8,128)(2,1)} %param.6) | copy-start | bytes 6291460
Sparse Core Ops, SparseCore 0:
  99.7 61.2 all-reduce.2
  163.6 92.3 reduce-scatter.1
where the time goes:
time: 268 us; the launch traced here: 267 us
  waiting for transfers between devices  113 us (42%)
  blocking collectives  64.7 us (24%)
  matrix products  35.1 us (13%)
  starting transfers between devices  15.7 us (6%)
  between operations  14.2 us (5%)
  local copies, waits for them, and re-layouts  13.7 us (5%)
  other arithmetic  10.8 us (4%)
    unnamed x1, blocking collectives  64.7 us
    all_to_all x1, waiting for transfers between devices, local(): lax.all_to_all(delta_slots, 'replica', split_axis=0, concat_axis=0, tiled...  55.8 us
    psum x1, waiting for transfers between devices, local(): low_rank = lax.psum(partial_low.astype(jnp.bfloat16), 'tensor')  33.4 us
    dot_general x1, matrix products, local(): jnp.dot(attended, out_weight, preferred_element_type=jnp.float32)  25.8 us
    reduce_scatter x1, waiting for transfers between devices, local(): lax.psum_scatter(partial_out.astype(jnp.bfloat16), 'tensor', scatter_dime...  23.6 us
    all_to_all x1, starting transfers between devices, local(): lax.all_to_all(outgoing, 'replica', split_axis=0, concat_axis=0, tiled=True)  8.78 us
    all_to_all x1, starting transfers between devices, local(): lax.all_to_all(delta_slots, 'replica', split_axis=0, concat_axis=0, tiled...  6.88 us
  transfers between devices with their start and end apart: 4, of which 3 were waited for; matrix products, arithmetic and copies ran while one was open for 15% of the time, Pallas kernels for 0%

commit v1 on v0

--- a/solution.py
+++ b/solution.py
@@ -41,7 +41,7 @@
     partial_low = jnp.einsum(
         "scbp,scrp->scrb", arrived, shrink_weight[served_ids], preferred_element_type=jnp.float32
     )
-    low_rank = lax.psum(partial_low.astype(jnp.bfloat16), "tensor")
+    low_rank = jnp.sum(lax.all_gather(partial_low.astype(jnp.bfloat16), "tensor"), axis=0)
     delta_slots = jnp.einsum(
         "scrb,scrp->scbp", low_rank, expand_weight[served_ids], preferred_element_type=jnp.float32
     ).astype(jnp.bfloat16)

time: 268 us -> 234 us (0.87)
  waiting for transfers between devices: 113 us -> 78.2 us
    psum x1 -> x0, waiting for transfers between devices: 33.4 us -> none  [local(): low_rank = lax.psum(partial_low.astype(jnp.bfloat16), 'tensor')]
    reduce_scatter x1, waiting for transfers between devices: 23.6 us -> 17.4 us  [local(): lax.psum_scatter(partial_out.astype(jnp.bfloat16), 'tensor', scatter_dime...]
    all_to_all x1, waiting for transfers between devices: 55.8 us -> 59.5 us  [local(): lax.all_to_all(delta_slots, 'replica', split_axis=0, concat_axis=0, tiled...]
  transfers between devices with their start and end apart: 4 -> 4, of which waited for: 3 -> 3; matrix products, arithmetic and copies ran while one was open for 15% -> 18% of each run, Pallas kernels for 0% -> 0%
where the time goes in v1:
time: 234 us
  waiting for transfers between devices  78.2 us (33%)
  blocking collectives  64.7 us (28%)
  matrix products  34.2 us (15%)
  starting transfers between devices  15.7 us (7%)
  between operations  14.2 us (6%)
  local copies, waits for them, and re-layouts  13.7 us (6%)
  other arithmetic  12.7 us (5%)
    unnamed x1, blocking collectives  64.7 us
    all_to_all x1, waiting for transfers between devices, local(): lax.all_to_all(delta_slots, 'replica', split_axis=0, concat_axis=0, tiled...  59.5 us
    dot_general x1, matrix products, local(): jnp.dot(attended, out_weight, preferred_element_type=jnp.float32)  25.8 us
    reduce_scatter x1, waiting for transfers between devices, local(): lax.psum_scatter(partial_out.astype(jnp.bfloat16), 'tensor', scatter_dime...  17.4 us
    all_to_all x1, starting transfers between devices, local(): lax.all_to_all(outgoing, 'replica', split_axis=0, concat_axis=0, tiled=True)  8.78 us
    all_to_all x1, starting transfers between devices, local(): lax.all_to_all(delta_slots, 'replica', split_axis=0, concat_axis=0, tiled...  6.88 us
    dot_general x1, matrix products, local(): jnp.einsum('scbp,scrp->scrb', arrived, shrink_weight[served_ids], preferr...  5.09 us
  transfers between devices with their start and end apart: 4, of which 3 were waited for; matrix products, arithmetic and copies ran while one was open for 18% of the time, Pallas kernels for 0%

profile of v1, /device:TPU:1, one launch (start us, length us, event | category | flops | bytes accessed | tf_op | source)
XLA Modules:
  0.0 233.5 jit_solution(6105414466722782579)
XLA Ops:
  6.5 0.8 and_select_fusion
  7.4 0.2 convert_reduce_fusion.1
  7.5 0.7 compare_select_fusion
  8.2 0.1 select_reduce_fusion
  8.3 0.1 fusion.7
  8.4 2.8 %gather_fusion.1 = bf16[16,128,1024]{2,1,0:T(8,128)(2,1)} fusion(bf16[8,128,1024]{2,1,0:T(8,128)(2,1)S(1)} %bitcast.33, s32[1024]{0:T(1024)S(1)} %pad_clamp_fusion.1), kind=kCustom, calls=%fused_computation.1 | custom fusion | bytes 8388672 | tf_op jit(solution)/shard_map/gather | solution.py:38
  11.2 4.5 %bitcast_select_fusion = bf16[16,1,128,1024]{3,2,1,0:T(8,128)(2,1)} fusion(bf16[16,128,1024]{2,1,0:T(8,128)(2,1)} %gather_fusion.1, pred[16]{0:T(512)(128)(4,1)S(1)} %fusion.7), kind=kLoop, calls=%fused_computation.10 | loop fusion | flops 2097152 | bytes 8388624 | tf_op jit(solution)/shard_map/jit(_where)/select_n | solution.py:38
  15.7 8.8 %all-to-all-start = ((bf16[16,1,128,1024]{3,2,1,0:T(8,128)(2,1)}), bf16[16,1,128,1024]{3,2,1,0:T(8,128)(2,1)}, u32[]{:S(2)}, u32[]{:S(2)}) async-start(bf16[16,1,128,1024]{3,2,1,0:T(8,128)(2,1)} %bitcast_select_fusion), calls=%async_computation.1 | async-start | bytes 8388608 | tf_op jit(solution)/shard_map/all_to_all | solution.py:40
  24.5 0.0 all-gather.3.cloned.1.call-start
  24.5 0.6 dynamic-slice
  25.8 0.2 dynamic-update-slice
  26.0 64.7 %all-reduce = s32[128]{0:T(128)S(1)} all-reduce(s32[128]{0:T(128)S(1)} %dynamic-update-slice), channel_id=1, replica_groups=mesh['replica'=16,'tensor'=8] {'replica'}, use_global_device_ids=true, to_apply=%add | all-reduce | flops 128 | bytes 1024
  90.8 0.1 reshape.154
  90.9 0.1 copy.8
  91.0 0.1 convert_reduce_fusion
  91.1 3.4 %gather_fusion = bf16[16,64,1024]{2,1,0:T(8,128)(2,1)} fusion(bf16[12,64,1024]{2,1,0:T(8,128)(2,1)} %param.8, s32[1024]{0:T(1024)S(1)} %pad_clamp_fusion.2), kind=kCustom, calls=%fused_computation | custom fusion | bytes 4194368 | tf_op jit(solution)/shard_map/gather | solution.py:42
  94.5 0.0 all-to-all-done
  94.5 5.1 %fusion.4 = bf16[16,64,128]{2,1,0:T(8,128)(2,1)} fusion(bf16[16,64,1024]{2,1,0:T(8,128)(2,1)} %gather_fusion, bf16[16,1,128,1024]{3,2,1,0:T(8,128)(2,1)} %all-to-all-done), kind=kOutput, calls=%fused_computation.12 | convolution fusion | flops 268566528 | bytes 6553600 | tf_op jit(solution)/shard_map/scbp,scrp->scrb/dot_general | solution.py:41
  99.6 0.0 all-gather.3.cloned.1.call-update
  99.6 0.0 reduce-scatter.2.cloned.1.call-start
  99.7 25.8 %convolution_convert_fusion = bf16[1024,8192]{1,0:T(8,128)(2,1)} fusion(bf16[1024,1024]{1,0:T(8,128)(2,1)S(1)} %copy-done, bf16[1024,8192]{1,0:T(8,128)(2,1)} %param.7), kind=kOutput, calls=%fused_computation.4 | convolution fusion | flops 17188257792 | bytes 35651584 | tf_op jit(solution)/shard_map/dot_general | solution.py:50
  125.5 0.0 reduce-scatter.2.cloned.1.call-update
  125.5 2.1 gather_fusion.2
  127.6 1.3 all-gather.3.cloned.1.call-done
  128.9 2.0 reduce.3
  130.9 3.3 %convert_bitcast_fusion = bf16[16,1,128,1024]{3,2,1,0:T(8,128)(2,1)} fusion(bf16[16,64,128]{2,1,0:T(8,128)(2,1)S(1)} %reduce.3, bf16[16,64,1024]{2,1,0:T(8,128)(2,1)S(1)} %gather_fusion.2), kind=kOutput, calls=%fused_computation.11 | convolution fusion | flops 270532608 | bytes 6553600 | tf_op jit(solution)/shard_map/scrb,scrp->scbp/dot_general | solution.py:45
  134.1 6.9 %all-to-all-start.1 = ((bf16[16,1,128,1024]{3,2,1,0:T(8,128)(2,1)}), bf16[16,1,128,1024]{3,2,1,0:T(8,128)(2,1)}, u32[]{:S(2)}, u32[]{:S(2)}) async-start(bf16[16,1,128,1024]{3,2,1,0:T(8,128)(2,1)} %convert_bitcast_fusion), calls=%async_computation.2 | async-start | bytes 8388608 | tf_op jit(solution)/shard_map/all_to_all | solution.py:48
  141.1 0.1 fusion.8
  141.1 59.5 %all-to-all-done.1 = bf16[16,1,128,1024]{3,2,1,0:T(8,128)(2,1)} async-done(((bf16[16,1,128,1024]{3,2,1,0:T(8,128)(2,1)}), bf16[16,1,128,1024]{3,2,1,0:T(8,128)(2,1)}, u32[]{:S(2)}, u32[]{:S(2)}) %all-to-all-start.1) | async-done | bytes 4194336 | tf_op jit(solution)/shard_map/all_to_all | solution.py:48
  200.6 4.4 %gather_fusion.3 = bf16[8,128,1024]{2,1,0:T(8,128)(2,1)} fusion(bf16[16,128,1024]{2,1,0:T(8,128)(2,1)} %bitcast.12, s32[1024]{0:T(1024)S(1)} %pad_clamp_fusion), kind=kCustom, calls=%fused_computation.3 | custom fusion | bytes 4194336 | tf_op jit(solution)/shard_map/gather | solution.py:49
  205.0 17.4 %reduce-scatter.2.cloned.1.call-done = bf16[1024,1024]{1,0:T(8,128)(2,1)} async-done(((bf16[1024,8192]{1,0:T(8,128)(2,1)}), bf16[1024,1024]{1,0:T(8,128)(2,1)}) %reduce-scatter.2.cloned.1.call-update) | async-done | bytes 2097168 | tf_op jit(solution)/shard_map/reduce_scatter | solution.py:51
  222.5 4.2 %fusion.1 = bf16[1024,1024]{1,0:T(8,128)(2,1)} fusion(bf16[1024,1024]{1,0:T(8,128)(2,1)} %reduce-scatter.2.cloned.1.call-done, bf16[8,128,1024]{2,1,0:T(8,128)(2,1)} %gather_fusion.3, pred[1024]{0:T(1024)(128)(4,1)S(1)} %fusion.8), kind=kLoop, calls=%fused_computation.7 | loop fusion | flops 5242880 | bytes 6292480 | tf_op jit(solution)/shard_map/convert_element_type | solution.py:58
  (19 shorter events, 0.1 us)
Async XLA Ops:
  6.5 1.9 copy-start
  15.7 8.9 %copy-start.4 = (u32[128]{0:T(128)S(1)}, u32[128]{0:T(128)}, u32[]{:S(2)}) copy-start(u32[128]{0:T(128)} %constant.45) | copy-start | bytes 1540
  15.7 10.1 %copy-start.2 = (s32[8]{0:T(128)S(1)}, s32[8]{0:T(128)}, u32[]{:S(2)}) copy-start(s32[8]{0:T(128)} %param.10) | copy-start | bytes 100
  15.7 78.8 %all-to-all-start = ((bf16[16,1,128,1024]{3,2,1,0:T(8,128)(2,1)}), bf16[16,1,128,1024]{3,2,1,0:T(8,128)(2,1)}, u32[]{:S(2)}, u32[]{:S(2)}) async-start(bf16[16,1,128,1024]{3,2,1,0:T(8,128)(2,1)} %bitcast_select_fusion), calls=%async_computation.1 | async-start | bytes 8388608 | tf_op jit(solution)/shard_map/all_to_all | solution.py:40
  24.5 104.4 %all-gather.3.cloned.1.call-start = ((), (), s32[]{:S(2)}) async-start(), calls=%async_computation.4 | async-start | bytes 2359296 | tf_op jit(solution)/shard_map/all_gather | solution.py:44
  99.6 122.8 %reduce-scatter.2.cloned.1.call-start = ((), (), s32[]{:S(2)}) async-start(), calls=%async_computation.3 | async-start | bytes 18874368 | tf_op jit(solution)/shard_map/reduce_scatter | solution.py:51
  134.1 6.9 %copy-start.3 = (s32[8]{0:T(128)S(1)}, s32[8]{0:T(128)}, u32[]{:S(2)}) copy-start(s32[8]{0:T(128)} %param.11) | copy-start | bytes 100
  134.1 66.5 %all-to-all-start.1 = ((bf16[16,1,128,1024]{3,2,1,0:T(8,128)(2,1)}), bf16[16,1,128,1024]{3,2,1,0:T(8,128)(2,1)}, u32[]{:S(2)}, u32[]{:S(2)}) async-start(bf16[16,1,128,1024]{3,2,1,0:T(8,128)(2,1)} %convert_bitcast_fusion), calls=%async_computation.2 | async-start | bytes 8388608 | tf_op jit(solution)/shard_map/all_to_all | solution.py:48
  200.6 26.1 %copy-start.1 = (bf16[1024,1024]{1,0:T(8,128)(2,1)S(1)}, bf16[1024,1024]{1,0:T(8,128)(2,1)}, u32[]{:S(2)}) copy-start(bf16[1024,1024]{1,0:T(8,128)(2,1)} %param.6) | copy-start | bytes 6291460
Sparse Core Ops, SparseCore 0:
  99.8 29.1 all-gather.2
  131.4 91.0 reduce-scatter.1
